TPU v7x, 512 devices: a whole 4x4x16 slice. The times are simulated.
512 devices in a mesh: ex: 64 (over y_lo, z, core), hid: 8 (over x, y_hi).
Axes of the slice: x: 4, y: 4 (y_hi: 2, y_lo: 2; y = y_hi * 2 + y_lo), z: 16, core: 2. Of those that a mesh axis runs over, the one named last changes fastest.
Arguments:
- activations: bfloat16 [256, 192, 14336], P('ex', None, 'hid'), may hold values from -6 to 6
- out_grads: bfloat16 [256, 192, 4096], P('ex', None, 'hid'), may hold values from -6 to 6
- token_mask: int32 [256, 192], P('ex'), may hold values from 0 to 1, as said below
- proj_in: bfloat16 [14336, 64], P('hid'), may hold values from -0.046875 to 0.046875
- proj_out: bfloat16 [4096, 64], P('hid'), may hold values from -0.09375 to 0.09375
- inv_input: float32 [64, 64], replicated, as said below
- inv_output: float32 [64, 64], replicated, as said below
- query_feats: bfloat16 [4096, 4096], P('ex', 'hid'), may hold values from -6 to 6
Outputs:
- scores: float32 [4096, 256], P('ex', 'hid')
Inputs may be any that keep to these rules, and one draw needn't show every extreme that they name: `token_mask`: each row is 48 or more ones followed by zeros; some row is all ones. `inv_input`: symmetric. `inv_output`: symmetric.
All inputs are finite; a program needn't handle non-finite values.
Results may differ from a plain program's by a relative error of at most 0.0041.
Values may be sent and summed in bfloat16 or wider, within the bound.
A program may use at most 64 MiB of HBM per device.

v0:
```python
import jax
import jax.numpy as jnp
from jax import lax
from jax.sharding import PartitionSpec as P


def local(
    activations, out_grads, token_mask, proj_in, proj_out, inv_input, inv_output, query_feats
):
    seq_count, length, unit_local = activations.shape
    rank_width = proj_in.shape[1]
    hid_size = lax.axis_size("hid")
    row_block = rank_width // hid_size
    my_index = lax.axis_index("hid")
    in_part = jnp.dot(
        activations.reshape(seq_count * length, unit_local),
        proj_in,
        preferred_element_type=jnp.float32,
    )
    in_part = jnp.dot(in_part, inv_input, precision=lax.Precision.HIGHEST)
    out_part = jnp.dot(
        out_grads.reshape(seq_count * length, out_grads.shape[2]),
        proj_out,
        preferred_element_type=jnp.float32,
    )
    token_weight = token_mask.astype(jnp.float32)
    tok_count = jnp.sum(token_weight, axis=1)
    in_full, out_full = lax.psum((in_part, out_part), "hid")
    in_mine = lax.dynamic_slice_in_dim(in_full, my_index * row_block, row_block, 1)
    masked = in_mine.reshape(seq_count, length, row_block) * token_weight[:, :, None]
    outer = jnp.einsum(
        "slr,slq->srq",
        masked,
        out_full.reshape(seq_count, length, rank_width),
        precision=lax.Precision.HIGHEST,
    )
    train_feats = (
        (outer / tok_count[:, None, None])
        .astype(jnp.bfloat16)
        .reshape(seq_count, row_block * rank_width)
    )
    query_count = query_feats.shape[0]
    queries = query_feats.reshape(query_count, row_block, rank_width).astype(jnp.float32)
    query_pre = jnp.einsum("qij,jk->qik", queries, inv_output, precision=lax.Precision.HIGHEST)
    query_pre = query_pre.astype(jnp.bfloat16).reshape(query_count, row_block * rank_width)
    partial_value = jnp.einsum(
        "qk,tk->qt",
        query_pre,
        lax.all_gather(train_feats, "ex", axis=0, tiled=True),
        preferred_element_type=jnp.float32,
    )
    return lax.psum_scatter(partial_value, "hid", scatter_dimension=1, tiled=True)


def solution(mesh):
    return jax.shard_map(
        local,
        mesh=mesh,
        in_specs=(
            P("ex", None, "hid"),
            P("ex", None, "hid"),
            P("ex", None),
            P("hid", None),
            P("hid", None),
            P(),
            P(),
            P("ex", "hid"),
        ),
        out_specs=P("ex", "hid"),
        check_vma=False,
    )
```

profile of v0, /device:TPU:2, one launch (start us, length us, event | category | flops | bytes accessed | tf_op | source)
XLA Modules:
  0.0 264.8 jit_solution(6362297296101887833)
XLA Ops:
  6.5 0.0 copy-start
  6.5 0.0 all-reduce.3.cloned.1.call-start
  6.5 1.6 fusion.6
  8.2 0.2 reshape.28
  8.4 0.0 copy-start.3
  8.4 0.7 copy.17
  9.2 0.0 copy-done
  9.2 0.0 copy-start.4
  9.2 0.0 copy-start.1
  9.2 0.0 copy-start.2
  9.2 1.9 fusion.4
  11.1 0.0 copy-done.3
  11.1 1.0 fusion.5
  12.2 0.0 all-reduce.3.cloned.1.call-update
  12.2 0.0 reduce-scatter.2.cloned.1.call-start
  12.2 0.0 copy-done.4
  12.3 0.0 copy-done.1
  12.3 0.1 reshape.23
  12.4 0.0 copy-done.2
  12.4 0.2 convolution_convert_fusion
  12.7 0.1 copy.16
  12.8 0.1 reshape.24
  12.9 0.1 convert_reduce_fusion
  13.0 103.1 %all-reduce.3.cloned.1.call-done = (f32[4,192,64]{1,2,0:T(8,128)}, f32[768,64]{0,1:T(8,128)}) async-done(((f32[4,192,64]{1,2,0:T(8,128)}, f32[768,64]{0,1:T(8,128)}), (f32[4,192,64]{1,2,0:T(8,128)}, f32[768,64]{0,1:T(8,128)})) %all-reduce.3.cloned.1.call-update) | async-done | bytes 393232 | tf_op jit(solution)/shard_map/psum | solution.py:28
  116.1 0.7 constant_dynamic-slice_fusion
  116.9 0.1 reshape.26
  117.0 1.3 fusion
  118.3 0.1 reshape.30
  118.3 64.0 %all-gather = bf16[64,4,512]{2,1,0:T(4,128)(2,1)S(1)} all-gather(bf16[1,4,512]{2,1,0:T(4,128)(2,1)S(1)} %reshape.30), channel_id=1, replica_groups=mesh['ex'=64,'hid'=8] {'ex'}, dimensions={0}, use_global_device_ids=true | all-gather | bytes 266240 | tf_op jit(solution)/shard_map/all_gather | solution.py:49
  182.3 0.1 reshape.31
  182.4 0.9 fusion.7
  183.3 0.0 reduce-scatter.2.cloned.1.call-update
  183.3 74.7 %reduce-scatter.2.cloned.1.call-done = f32[64,32]{0,1:T(8,128)} async-done(((f32[64,256]{0,1:T(8,128)}), f32[64,32]{0,1:T(8,128)}) %reduce-scatter.2.cloned.1.call-update) | async-done | bytes 8208 | tf_op jit(solution)/shard_map/reduce_scatter | solution.py:52
  (3 shorter events, 0.0 us)
Async XLA Ops:
  6.5 2.6 copy-start
  6.5 109.6 %all-reduce.3.cloned.1.call-start = ((), (), s32[]{:S(2)}) async-start(), calls=%async_computation.2 | async-start | bytes 917504 | tf_op jit(solution)/shard_map/psum | solution.py:28
  8.4 2.7 %copy-start.3 = (f32[64,64]{1,0:T(8,128)S(1)}, f32[64,64]{1,0:T(8,128)}, u32[]{:S(2)}) copy-start(f32[64,64]{1,0:T(8,128)} %param.13) | copy-start | bytes 49156
  9.2 3.1 %copy-start.4 = (s32[4,192]{1,0:T(4,128)S(1)}, s32[4,192]{1,0:T(4,128)}, u32[]{:S(2)}) copy-start(s32[4,192]{1,0:T(4,128)} %param.10) | copy-start | bytes 9220
  9.2 3.1 %copy-start.1 = (bf16[64,512]{1,0:T(8,128)(2,1)S(1)}, bf16[64,512]{1,0:T(8,128)(2,1)}, u32[]{:S(2)}) copy-start(bf16[64,512]{1,0:T(8,128)(2,1)} %param.15) | copy-start | bytes 196612
  9.2 3.2 %copy-start.2 = (f32[64,64]{1,0:T(8,128)S(1)}, f32[64,64]{1,0:T(8,128)}, u32[]{:S(2)}) copy-start(f32[64,64]{1,0:T(8,128)} %param.14) | copy-start | bytes 49156
  12.2 245.8 %reduce-scatter.2.cloned.1.call-start = ((), (), s32[]{:S(2)}) async-start(), calls=%async_computation.1 | async-start | bytes 147456 | tf_op jit(solution)/shard_map/reduce_scatter | solution.py:52
Sparse Core Ops, SparseCore 0:
  12.3 103.7 all-reduce.2
  183.4 74.5 reduce-scatter.1
where the time goes:
time: 265 us
  waiting for transfers between devices  178 us (67%)
  blocking collectives  64 us (24%)
  between operations  13.5 us (5%)
  matrix products  6.98 us (3%)
    psum x1, waiting for transfers between devices, local(): in_full, out_full = lax.psum((in_part, out_part), 'hid')  103 us
    reduce_scatter x1, waiting for transfers between devices, local(): lax.psum_scatter(partial_value, 'hid', scatter_dimension=1, tiled=True)  74.7 us
    all_gather x1, blocking collectives, local(): lax.all_gather(train_feats, 'ex', axis=0, tiled=True)  64 us
  transfers between devices with their start and end apart: 2, of which 2 were waited for; matrix products, arithmetic and copies ran while one was open for 0% of the time, Pallas kernels for 0%

commit v1 on v0

--- a/solution.py
+++ b/solution.py
@@ -46,7 +46,12 @@
     partial_value = jnp.einsum(
         "qk,tk->qt",
         query_pre,
-        lax.all_gather(train_feats, "ex", axis=0, tiled=True),
+        jnp.concatenate(
+            lax.all_to_all(
+                jnp.stack([train_feats for _ in range(lax.axis_size("ex"))]), "ex", 0, 0
+            ),
+            axis=0,
+        ),
         preferred_element_type=jnp.float32,
     )
     return lax.psum_scatter(partial_value, "hid", scatter_dimension=1, tiled=True)

time: 265 us -> 239 us (0.902)
  blocking collectives: 64 us -> 0 us
  waiting for transfers between devices: 178 us -> 201 us
  starting transfers between devices: 0.04 us -> 13.3 us
    all_gather x1 -> x0, blocking collectives: 64 us -> none  [local(): lax.all_gather(train_feats, 'ex', axis=0, tiled=True)]
    all_to_all x0 -> x1, waiting for transfers between devices: none -> 20.7 us  [local(): lax.all_to_all(jnp.stack([train_feats for _ in range(lax.axis_size('ex'))...]
    all_to_all x0 -> x1, starting transfers between devices: none -> 13.2 us  [local(): lax.all_to_all(jnp.stack([train_feats for _ in range(lax.axis_size('ex'))...]
  transfers between devices with their start and end apart: 2 -> 3, of which waited for: 2 -> 3; matrix products, arithmetic and copies ran while one was open for 0% -> 0% of each run, Pallas kernels for 0% -> 0%
where the time goes in v1:
time: 239 us; the launch traced here: 238 us
  waiting for transfers between devices  201 us (84%)
  between operations  13.5 us (6%)
  starting transfers between devices  13.3 us (6%)
  matrix products  7.13 us (3%)
  local copies, waits for them, and re-layouts  3.11 us (1%)
    psum x1, waiting for transfers between devices, local(): in_full, out_full = lax.psum((in_part, out_part), 'hid')  104 us
    reduce_scatter x1, waiting for transfers between devices, local(): lax.psum_scatter(partial_value, 'hid', scatter_dimension=1, tiled=True)  76.8 us
    all_to_all x1, waiting for transfers between devices, local(): lax.all_to_all(jnp.stack([train_feats for _ in range(lax.axis_size('ex'))...  20.7 us
    all_to_all x1, starting transfers between devices, local(): lax.all_to_all(jnp.stack([train_feats for _ in range(lax.axis_size('ex'))...  13.2 us
  transfers between devices with their start and end apart: 3, of which 3 were waited for; matrix products, arithmetic and copies ran while one was open for 0% of the time, Pallas kernels for 0%

profile of v1, /device:TPU:2, one launch (start us, length us, event | category | flops | bytes accessed | tf_op | source)
XLA Modules:
  0.0 238.5 jit_solution(5738096975588881693)
XLA Ops:
  6.5 0.0 copy-start
  6.5 0.0 all-reduce.3.cloned.1.call-start
  6.5 1.6 fusion.6
  8.2 0.2 reshape.30
  8.4 0.7 copy.13
  9.1 0.0 copy-done
  9.1 0.0 copy-start.2
  9.1 0.0 copy-start.4
  9.1 0.0 copy-start.1
  9.1 0.0 copy-start.3
  9.2 1.8 fusion.4
  11.0 0.0 copy-done.2
  11.0 1.3 fusion.5
  12.3 0.0 all-reduce.3.cloned.1.call-update
  12.3 0.0 copy-done.4
  12.3 0.1 convert_reduce_fusion
  12.5 103.8 %all-reduce.3.cloned.1.call-done = (f32[4,192,64]{1,2,0:T(8,128)}, f32[768,64]{0,1:T(8,128)}) async-done(((f32[4,192,64]{1,2,0:T(8,128)}, f32[768,64]{0,1:T(8,128)}), (f32[4,192,64]{1,2,0:T(8,128)}, f32[768,64]{0,1:T(8,128)})) %all-reduce.3.cloned.1.call-update) | async-done | bytes 393232 | tf_op jit(solution)/shard_map/psum | solution.py:28
  116.3 0.7 constant_dynamic-slice_fusion
  117.0 0.1 reshape.28
  117.2 1.3 fusion
  118.4 0.1 stack_reshape.2
  118.5 0.8 stack.3
  119.3 13.2 %all-to-all-start = ((bf16[64,4,512]{2,1,0:T(4,128)(2,1)}), bf16[64,4,512]{2,1,0:T(4,128)(2,1)S(1)}, u32[]{:S(2)}, u32[]{:S(2)}) async-start(bf16[64,4,512]{2,1,0:T(4,128)(2,1)} %stack.3), calls=%async_computation | async-start | bytes 524288 | tf_op jit(solution)/shard_map/all_to_all | solution.py:50
  132.5 0.0 reduce-scatter.2.cloned.1.call-start
  132.6 0.0 copy-done.1
  132.6 0.1 reshape.25
  132.7 0.0 copy-done.3
  132.7 0.2 convolution_convert_fusion
  133.0 0.1 copy.12
  133.1 0.1 reshape.26
  133.2 20.7 %all-to-all-done = bf16[64,4,512]{2,1,0:T(4,128)(2,1)S(1)} async-done(((bf16[64,4,512]{2,1,0:T(4,128)(2,1)}), bf16[64,4,512]{2,1,0:T(4,128)(2,1)S(1)}, u32[]{:S(2)}, u32[]{:S(2)}) %all-to-all-start) | async-done | bytes 262176 | tf_op jit(solution)/shard_map/all_to_all | solution.py:50
  153.9 0.1 reshape.31
  154.0 0.9 fusion.7
  154.8 0.0 reduce-scatter.2.cloned.1.call-update
  154.9 76.8 %reduce-scatter.2.cloned.1.call-done = f32[64,32]{0,1:T(8,128)} async-done(((f32[64,256]{0,1:T(8,128)}), f32[64,32]{0,1:T(8,128)}) %reduce-scatter.2.cloned.1.call-update) | async-done | bytes 8208 | tf_op jit(solution)/shard_map/reduce_scatter | solution.py:57
  (3 shorter events, 0.0 us)
Async XLA Ops:
  6.5 2.6 %copy-start = (bf16[4,192,1792]{2,1,0:T(8,128)(2,1)S(1)}, bf16[4,192,1792]{2,1,0:T(8,128)(2,1)}, u32[]{:S(2)}) copy-start(bf16[4,192,1792]{2,1,0:T(8,128)(2,1)} %param.8) | copy-start | bytes 8257540
  6.5 109.8 %all-reduce.3.cloned.1.call-start = ((), (), s32[]{:S(2)}) async-start(), calls=%async_computation.3 | async-start | bytes 917504 | tf_op jit(solution)/shard_map/psum | solution.py:28
  9.1 1.9 copy-start.2
  9.1 3.2 %copy-start.4 = (s32[4,192]{1,0:T(4,128)S(1)}, s32[4,192]{1,0:T(4,128)}, u32[]{:S(2)}) copy-start(s32[4,192]{1,0:T(4,128)} %param.10) | copy-start | bytes 9220
  9.1 123.4 %copy-start.1 = (bf16[64,512]{1,0:T(8,128)(2,1)S(1)}, bf16[64,512]{1,0:T(8,128)(2,1)}, u32[]{:S(2)}) copy-start(bf16[64,512]{1,0:T(8,128)(2,1)} %param.15) | copy-start | bytes 196612
  9.1 123.6 %copy-start.3 = (f32[64,64]{1,0:T(8,128)S(1)}, f32[64,64]{1,0:T(8,128)}, u32[]{:S(2)}) copy-start(f32[64,64]{1,0:T(8,128)} %param.14) | copy-start | bytes 49156
  119.3 34.6 %all-to-all-start = ((bf16[64,4,512]{2,1,0:T(4,128)(2,1)}), bf16[64,4,512]{2,1,0:T(4,128)(2,1)S(1)}, u32[]{:S(2)}, u32[]{:S(2)}) async-start(bf16[64,4,512]{2,1,0:T(4,128)(2,1)} %stack.3), calls=%async_computation | async-start | bytes 524288 | tf_op jit(solution)/shard_map/all_to_all | solution.py:50
  132.5 99.1 %reduce-scatter.2.cloned.1.call-start = ((), (), s32[]{:S(2)}) async-start(), calls=%async_computation.2 | async-start | bytes 147456 | tf_op jit(solution)/shard_map/reduce_scatter | solution.py:57
Sparse Core Ops, SparseCore 0:
  12.4 103.8 all-reduce.2
  155.0 76.6 reduce-scatter.1
